TPU v7x, 32 devices: a whole 2x2x4 slice. The times are simulated.
32 devices in a mesh: groups: 2 (over y), seq: 4 (over z), adapt: 4 (over x, core).
Axes of the slice: x: 2, y: 2, z: 4, core: 2. Of those that a mesh axis runs over, the one named last changes fastest.
Arguments:
- image: bfloat16 [16, 2048, 3072], P(('groups', 'adapt'), 'seq'), parts along dimension 0, may hold values from -6 to 6
- modulation: float32 [16, 2, 3072], P(('groups', 'adapt')), parts along dimension 0, may hold values from -3 to 3
- query_key_value_weight: bfloat16 [3072, 6144], P(None, 'adapt'), may hold values from -0.109375 to 0.109375
- pooled_down_factor: bfloat16 [16, 3072, 64], P('seq'), may hold values from -0.109375 to 0.109375
- pooled_up_factor: bfloat16 [16, 64, 6144], P('seq', None, 'adapt'), may hold values from -0.75 to 0.75
- request_adapter: int32 [16], P('groups'), parts along dimension 0, may hold values from 0 to 15
- adapter_slot_table: int32 [16], replicated, may hold values from 0 to 15, each once
- row_request: int32 [16], P('groups'), parts along dimension 0, may hold values from 0 to 7, each once
- text_key_value: bfloat16 [16, 512, 2, 2048], P('groups', 'seq', None, 'adapt'), parts along dimension 0, may hold values from -110 to 110
- query_key_gain: float32 [2, 128], replicated, may hold values from 1 to 2.5
Outputs:
- attended: bfloat16 [16, 2048, 2048], P('groups', 'seq', 'adapt'), parts along dimension 0
There are 2 independent parts, one for each index of `groups`. A program takes and returns all parts, laid end to end along the dimension named above; an argument that names none is the same for every part. Nothing has to cross between parts.
All inputs are finite; a program needn't handle non-finite values.
Results may differ from a plain program's by a relative error of at most 0.0049.
The roundings to bfloat16 on the way count: a program that leaves them out, or rounds other values in their place, can miss the bound.
Values may be sent and summed in bfloat16 or wider, within the bound.
A program may use at most 192 MiB of HBM per device.

v0:
```python
import math
import jax
import jax.numpy as jnp
from jax import lax
from jax.sharding import PartitionSpec as P

HEAD_SIZE = 128


def layer_modulate(image, modulation):
    widened = image.astype(jnp.float32)
    centre = widened - jnp.mean(widened, axis=-1, keepdims=True)
    variance = jnp.mean(centre * centre, axis=-1, keepdims=True)
    normed = centre * lax.rsqrt(variance + 1e-06)
    return ((1.0 + modulation[:, 1, None, :]) * normed + modulation[:, 0, None, :]).astype(
        jnp.bfloat16
    )


def rms_scale(values, gain):
    return values * lax.rsqrt(jnp.mean(values * values, axis=-1, keepdims=True) + 1e-06) * gain


def attend_item(operands):
    queries, joined = operands
    key_rows = joined[:, 0]
    value_rows = joined[:, 1]
    query_count = queries.shape[0]
    block = math.gcd(query_count, 512)
    inverse = 1.0 / math.sqrt(queries.shape[-1])
    blocked = queries.reshape(query_count // block, block, queries.shape[-1])

    def one_block(block_rows):
        scores = (
            lax.dot_general(
                block_rows, key_rows, (((1,), (1,)), ((), ())), preferred_element_type=jnp.float32
            )
            * inverse
        )
        highest = jnp.max(scores, axis=-1, keepdims=True)
        weights = jnp.exp(scores - highest)
        weights = weights / jnp.sum(weights, axis=-1, keepdims=True)
        return jnp.dot(
            weights.astype(jnp.bfloat16), value_rows, preferred_element_type=jnp.float32
        ).astype(jnp.bfloat16)

    return lax.map(one_block, blocked).reshape(queries.shape)


def on_device(
    image,
    modulation,
    query_key_value_weight,
    pooled_down_factor,
    pooled_up_factor,
    request_adapter,
    adapter_slot_table,
    row_request,
    text_key_value,
    query_key_gain,
):
    seq_index = lax.axis_index("seq")
    all_requests = request_adapter.shape[0]
    local_pool_slice = pooled_down_factor.shape[0]
    pool_total = adapter_slot_table.shape[0]
    heads_local = query_key_value_weight.shape[1] // (3 * HEAD_SIZE)
    text_local = text_key_value.shape[1]
    modulated = layer_modulate(image, modulation)
    request_match = row_request[:, None] == jnp.arange(all_requests, dtype=jnp.int32)[None, :]
    chosen_ids = jnp.sum(jnp.where(request_match, request_adapter[None, :], 0), axis=1)
    slot_match = chosen_ids[:, None] == jnp.arange(pool_total, dtype=jnp.int32)[None, :]
    slots = jnp.sum(jnp.where(slot_match, adapter_slot_table[None, :], 0), axis=1)
    owned = slots // local_pool_slice == seq_index
    local_match = (slots % local_pool_slice)[:, None] == jnp.arange(
        local_pool_slice, dtype=jnp.int32
    )[None, :]
    slot_picker = (owned[:, None] & local_match).astype(jnp.bfloat16)
    up_terms = jnp.einsum(
        "eq,qfx->efx", slot_picker, pooled_up_factor, preferred_element_type=jnp.float32
    ).astype(jnp.bfloat16)
    down_terms = jnp.einsum(
        "mv,vna->mna", slot_picker, pooled_down_factor, preferred_element_type=jnp.float32
    ).astype(jnp.bfloat16)
    down_fetched, up_fetched = (
        lax.psum(down_terms, "seq").astype(jnp.float32),
        lax.psum(up_terms, "seq").astype(jnp.float32),
    )
    down_fetched = down_fetched.astype(jnp.bfloat16)
    up_fetched = up_fetched.astype(jnp.bfloat16)
    block_rows = lax.all_gather(modulated, "adapt", axis=0, tiled=True)
    shrunk = jnp.einsum(
        "rtd,rdk->rtk", block_rows, down_fetched, preferred_element_type=jnp.float32
    ).astype(jnp.bfloat16)
    frozen = jnp.einsum(
        "rtd,dc->rtc", block_rows, query_key_value_weight, preferred_element_type=jnp.float32
    )
    qkv = frozen + jnp.einsum(
        "rtk,rkc->rtc", shrunk, up_fetched, preferred_element_type=jnp.float32
    )
    token_local = qkv.shape[1]
    qkv = qkv.reshape(all_requests, token_local, heads_local, 3, HEAD_SIZE)
    queries = rms_scale(qkv[:, :, :, 0], query_key_gain[0]).astype(jnp.bfloat16)
    image_keys = rms_scale(qkv[:, :, :, 1], query_key_gain[1]).astype(jnp.bfloat16)
    image_values = qkv[:, :, :, 2].astype(jnp.bfloat16)
    image_pairs = jnp.transpose(jnp.stack([image_keys, image_values], axis=3), (0, 2, 1, 3, 4))
    text_pairs = jnp.transpose(
        text_key_value.reshape(all_requests, text_local, 2, heads_local, HEAD_SIZE), (0, 3, 1, 2, 4)
    )
    joined = jnp.concatenate([image_pairs, text_pairs], axis=2)
    joined = joined.reshape(all_requests * heads_local, token_local + text_local, 2, HEAD_SIZE)
    queries = jnp.transpose(queries, (0, 2, 1, 3)).reshape(
        all_requests * heads_local, token_local, HEAD_SIZE
    )
    query_items, joined_items = (
        lax.all_to_all(queries, "seq", split_axis=0, concat_axis=1, tiled=True),
        lax.all_to_all(joined, "seq", split_axis=0, concat_axis=1, tiled=True),
    )
    attended = lax.map(attend_item, (query_items, joined_items))
    returned = lax.all_to_all(attended, "seq", split_axis=1, concat_axis=0, tiled=True)
    returned = returned.reshape(all_requests, heads_local, token_local, HEAD_SIZE)
    return jnp.transpose(returned, (0, 2, 1, 3)).reshape(
        all_requests, token_local, heads_local * HEAD_SIZE
    )


def solution(mesh):
    in_specs = (
        P(("groups", "adapt"), "seq", None),
        P(("groups", "adapt"), None, None),
        P(None, "adapt"),
        P("seq", None, None),
        P("seq", None, "adapt"),
        P("groups"),
        P(),
        P("groups"),
        P("groups", "seq", None, "adapt"),
        P(),
    )
    out_specs = P("groups", "seq", "adapt")
    return jax.shard_map(
        on_device, mesh=mesh, in_specs=in_specs, out_specs=out_specs, check_vma=False
    )
```

profile of v0, /device:TPU:0, one launch (start us, length us, event | category | flops | bytes accessed | tf_op | source)
XLA Modules:
  0.0 888.3 jit_solution(3175267230559958143)
XLA Ops:
  9.2 2.8 convolution_convert_fusion
  12.1 3.1 convolution_convert_fusion.1
  15.2 3.7 convert_reduce_fusion
  18.9 4.5 fusion.10
  23.6 9.4 %fusion.13 = bf16[2,512,3072]{2,1,0:T(8,128)(2,1)} fusion(bf16[2,512,3072]{2,1,0:T(8,128)(2,1)} %param.14, f32[2,3072]{1,0:T(2,128)S(1)} %get-tuple-element.83, f32[2,512]{1,0:T(2,128)S(1)} %add_rsqrt_fusion.2, f32[2,512]{1,0:T(2,128)S(1)} %broadcast_multiply_fusion, f32[2,3072]{1,0:T(2,128)S(1)} %get-tuple-element.84), kind=kLoop, calls=%fused_computation.24 | loop fusion | flops 18874368 | bytes 12640256 | tf_op jit(solution)/shard_map/convert_element_type | solution.py:15
  34.2 156.1 %all-reduce.3.cloned.1.call-done = (bf16[8,64,1536]{2,0,1:T(8,128)(2,1)}, bf16[8,3072,64]{1,0,2:T(8,128)(2,1)}) async-done(((bf16[8,64,1536]{2,0,1:T(8,128)(2,1)}, bf16[8,3072,64]{1,0,2:T(8,128)(2,1)}), (bf16[8,64,1536]{2,0,1:T(8,128)(2,1)}, bf16[8,3072,64]{1,0,2:T(8,128)(2,1)})) %all-reduce.3.cloned.1.call-update) | async-done | bytes 4718608 | tf_op jit(solution)/shard_map/psum | solution.py:86
  190.3 23.9 %fusion.18 = f32[8,512,1536]{2,1,0:T(8,128)} fusion(bf16[8,64,1536]{2,0,1:T(8,128)(2,1)} %get-tuple-element.73, bf16[8,512,3072]{2,1,0:T(8,128)(2,1)} %all-gather.2.cloned.1.call-done, bf16[8,3072,64]{1,0,2:T(8,128)(2,1)} %get-tuple-element.74), kind=kOutput, calls=%fused_computation.40 | convolution fusion | flops 2416181248 | bytes 55050240 | tf_op jit(solution)/shard_map/rtk,rkc->rtc/dot_general | solution.py:97
  214.3 47.6 %convolution_add_fusion = f32[8,512,1536]{2,1,0:T(8,128)} fusion(f32[8,512,1536]{2,1,0:T(8,128)} %fusion.18, bf16[8,512,3072]{2,1,0:T(8,128)(2,1)} %all-gather.2.cloned.1.call-done, bf16[3072,1536]{1,0:T(8,128)(2,1)} %param.16), kind=kOutput, calls=%fused_computation.16 | convolution fusion | flops 38660997120 | bytes 84934656 | tf_op jit(solution)/shard_map/rtd,dc->rtc/dot_general | solution.py:94
  261.9 24.7 %copy.49 = f32[8,512,1536]{1,2,0:T(8,128)} copy(f32[8,512,1536]{2,1,0:T(8,128)} %convolution_add_fusion) | data formatting | bytes 50331648 | tf_op jit(solution)/shard_map/add | solution.py:97
  286.6 4.6 multiply_reduce_fusion.1
  291.2 7.0 fusion.15
  298.2 6.5 copy.50
  304.6 5.2 all-to-all-start
  309.8 6.2 copy.52
  316.0 3.2 copy.79
  319.1 4.0 slice.55
  323.1 4.6 multiply_reduce_fusion
  327.8 7.0 multiply_convert_fusion
  334.7 6.2 maximum_bitcast_fusion
  340.9 9.1 %pad_maximum_fusion = bf16[8,4,640,2,128]{2,4,3,1,0:T(8,128)(2,1)} fusion(bf16[8,4,128,2,128]{2,4,3,1,0:T(8,128)(2,1)} %bitcast.102, bf16[8,4,512,2,128]{2,4,3,1,0:T(8,128)(2,1)} %maximum_bitcast_fusion), kind=kLoop, calls=%fused_computation.25 | loop fusion | flops 20971520 | bytes 20971520 | tf_op jit(solution)/shard_map/concatenate | solution.py:109
  350.1 15.1 %copy.54 = bf16[8,4,640,2,128]{4,2,3,1,0:T(8,128)(2,1)} copy(bf16[8,4,640,2,128]{2,4,3,1,0:T(8,128)(2,1)} %pad_maximum_fusion) | data formatting | bytes 20971520 | tf_op jit(solution)/shard_map/concatenate | solution.py:109
  365.2 38.2 %all-to-all-done = bf16[32,512,128]{2,1,0:T(8,128)(2,1)} async-done(((bf16[32,512,128]{2,1,0:T(8,128)(2,1)}), bf16[32,512,128]{2,1,0:T(8,128)(2,1)}, u32[]{:S(2)}, u32[]{:S(2)}) %all-to-all-start) | async-done | bytes 4194336 | tf_op jit(solution)/shard_map/all_to_all | solution.py:115
  403.3 6.0 all-to-all-start.1
  409.4 4.6 copy.51
  414.0 223.2 %all-to-all-done.1 = bf16[32,640,2,128]{3,1,2,0:T(8,128)(2,1)} async-done(((bf16[32,640,2,128]{3,1,2,0:T(8,128)(2,1)}), bf16[32,640,2,128]{3,1,2,0:T(8,128)(2,1)}, u32[]{:S(2)}, u32[]{:S(2)}) %all-to-all-start.1) | async-done | bytes 10485792 | tf_op jit(solution)/shard_map/all_to_all | solution.py:116
  637.1 9.2 %copy.55 = bf16[8,4,640,2,128]{4,2,1,3,0:T(8,128)(2,1)} copy(bf16[8,4,640,2,128]{4,2,3,0,1:T(8,128)(2,1)} %bitcast.23) | data formatting | bytes 20971520 | tf_op jit(solution)/shard_map/all_to_all | solution.py:116
  646.3 118.3 %while.21 = (s32[]{:T(128)}, bf16[8,2048,128]{2,1,0:T(8,128)(2,1)}, bf16[8,2048,128]{2,1,0:T(8,128)(2,1)}, bf16[8,2560,2,128]{3,1,2,0:T(8,128)(2,1)}, s32[]{:T(128)}, /*index=5*/s32[]{:T(128)}, s32[]{:T(128)}) while((s32[]{:T(128)}, bf16[8,2048,128]{2,1,0:T(8,128)(2,1)}, bf16[8,2048,128]{2,1,0:T(8,128)(2,1)}, ...), condition=%wide.region_13.14_spmd, body=%wide.region_8.13_spmd.sunk | while | flops 680328192 | bytes 24652504 | solution.py:118
  646.3 1.4 dynamic-slice_bitcast_fusion.2
  647.8 1.1 constant_dynamic-slice_fusion.2
  648.9 11.3 %while.22 = (s32[]{:T(128)}, bf16[4,512,128]{2,1,0:T(8,128)(2,1)S(1)}, bf16[4,512,128]{2,1,0:T(8,128)(2,1)S(1)}, bf16[2560,128]{1,0:T(8,128)(2,1)S(1)}, bf16[2560,128]{1,0:T(8,128)(2,1)S(1)}, /*index=5*/s32[]{:T(128)}) while((s32[]{:T(128)}, bf16[4,512,128]{2,1,0:T(8,128)(2,1)S(1)}, bf16[4,512,128]{2,1,0:T(8,128)(2,1)S(1)}, ...), condition=%wide.region_12.12_spmd, body=%wide.region_9.11_spmd.sunk | while | flops 680328192 | bytes 17311820 | solution.py:47
  653.6 1.0 fusion.46
  656.4 1.0 fusion.46
  659.2 1.0 fusion.46
  661.1 1.4 dynamic-slice_bitcast_fusion.2
  662.6 1.1 constant_dynamic-slice_fusion.2
  663.7 11.4 %while.22 = (s32[]{:T(128)}, bf16[4,512,128]{2,1,0:T(8,128)(2,1)S(1)}, bf16[4,512,128]{2,1,0:T(8,128)(2,1)S(1)}, bf16[2560,128]{1,0:T(8,128)(2,1)S(1)}, bf16[2560,128]{1,0:T(8,128)(2,1)S(1)}, /*index=5*/s32[]{:T(128)}) while((s32[]{:T(128)}, bf16[4,512,128]{2,1,0:T(8,128)(2,1)S(1)}, bf16[4,512,128]{2,1,0:T(8,128)(2,1)S(1)}, ...), condition=%wide.region_12.12_spmd, body=%wide.region_9.11_spmd.sunk | while | flops 680328192 | bytes 17311820 | solution.py:47
  668.3 1.0 fusion.46
  671.2 1.0 fusion.46
  674.0 1.0 fusion.46
  675.9 1.4 dynamic-slice_bitcast_fusion.2
  677.4 1.1 constant_dynamic-slice_fusion.2
  678.5 11.4 %while.22 = (s32[]{:T(128)}, bf16[4,512,128]{2,1,0:T(8,128)(2,1)S(1)}, bf16[4,512,128]{2,1,0:T(8,128)(2,1)S(1)}, bf16[2560,128]{1,0:T(8,128)(2,1)S(1)}, bf16[2560,128]{1,0:T(8,128)(2,1)S(1)}, /*index=5*/s32[]{:T(128)}) while((s32[]{:T(128)}, bf16[4,512,128]{2,1,0:T(8,128)(2,1)S(1)}, bf16[4,512,128]{2,1,0:T(8,128)(2,1)S(1)}, ...), condition=%wide.region_12.12_spmd, body=%wide.region_9.11_spmd.sunk | while | flops 680328192 | bytes 17311820 | solution.py:47
  680.3 1.0 fusion.46
  683.1 1.0 fusion.46
  690.7 1.4 dynamic-slice_bitcast_fusion.2
  692.2 1.1 constant_dynamic-slice_fusion.2
  693.3 11.4 %while.22 = (s32[]{:T(128)}, bf16[4,512,128]{2,1,0:T(8,128)(2,1)S(1)}, bf16[4,512,128]{2,1,0:T(8,128)(2,1)S(1)}, bf16[2560,128]{1,0:T(8,128)(2,1)S(1)}, bf16[2560,128]{1,0:T(8,128)(2,1)S(1)}, /*index=5*/s32[]{:T(128)}) while((s32[]{:T(128)}, bf16[4,512,128]{2,1,0:T(8,128)(2,1)S(1)}, bf16[4,512,128]{2,1,0:T(8,128)(2,1)S(1)}, ...), condition=%wide.region_12.12_spmd, body=%wide.region_9.11_spmd.sunk | while | flops 680328192 | bytes 17311820 | solution.py:47
  705.5 1.4 dynamic-slice_bitcast_fusion.2
  707.0 1.1 constant_dynamic-slice_fusion.2
  708.1 11.4 %while.22 = (s32[]{:T(128)}, bf16[4,512,128]{2,1,0:T(8,128)(2,1)S(1)}, bf16[4,512,128]{2,1,0:T(8,128)(2,1)S(1)}, bf16[2560,128]{1,0:T(8,128)(2,1)S(1)}, bf16[2560,128]{1,0:T(8,128)(2,1)S(1)}, /*index=5*/s32[]{:T(128)}) while((s32[]{:T(128)}, bf16[4,512,128]{2,1,0:T(8,128)(2,1)S(1)}, bf16[4,512,128]{2,1,0:T(8,128)(2,1)S(1)}, ...), condition=%wide.region_12.12_spmd, body=%wide.region_9.11_spmd.sunk | while | flops 680328192 | bytes 17311820 | solution.py:47
  720.3 1.4 dynamic-slice_bitcast_fusion.2
  721.8 1.1 constant_dynamic-slice_fusion.2
  722.9 11.4 %while.22 = (s32[]{:T(128)}, bf16[4,512,128]{2,1,0:T(8,128)(2,1)S(1)}, bf16[4,512,128]{2,1,0:T(8,128)(2,1)S(1)}, bf16[2560,128]{1,0:T(8,128)(2,1)S(1)}, bf16[2560,128]{1,0:T(8,128)(2,1)S(1)}, /*index=5*/s32[]{:T(128)}) while((s32[]{:T(128)}, bf16[4,512,128]{2,1,0:T(8,128)(2,1)S(1)}, bf16[4,512,128]{2,1,0:T(8,128)(2,1)S(1)}, ...), condition=%wide.region_12.12_spmd, body=%wide.region_9.11_spmd.sunk | while | flops 680328192 | bytes 17311820 | solution.py:47
  735.1 1.4 dynamic-slice_bitcast_fusion.2
  736.6 1.1 constant_dynamic-slice_fusion.2
  737.6 11.4 %while.22 = (s32[]{:T(128)}, bf16[4,512,128]{2,1,0:T(8,128)(2,1)S(1)}, bf16[4,512,128]{2,1,0:T(8,128)(2,1)S(1)}, bf16[2560,128]{1,0:T(8,128)(2,1)S(1)}, bf16[2560,128]{1,0:T(8,128)(2,1)S(1)}, /*index=5*/s32[]{:T(128)}) while((s32[]{:T(128)}, bf16[4,512,128]{2,1,0:T(8,128)(2,1)S(1)}, bf16[4,512,128]{2,1,0:T(8,128)(2,1)S(1)}, ...), condition=%wide.region_12.12_spmd, body=%wide.region_9.11_spmd.sunk | while | flops 680328192 | bytes 17311820 | solution.py:47
  749.8 1.4 dynamic-slice_bitcast_fusion.2
  751.3 1.1 constant_dynamic-slice_fusion.2
  752.4 11.4 %while.22 = (s32[]{:T(128)}, bf16[4,512,128]{2,1,0:T(8,128)(2,1)S(1)}, bf16[4,512,128]{2,1,0:T(8,128)(2,1)S(1)}, bf16[2560,128]{1,0:T(8,128)(2,1)S(1)}, bf16[2560,128]{1,0:T(8,128)(2,1)S(1)}, /*index=5*/s32[]{:T(128)}) while((s32[]{:T(128)}, bf16[4,512,128]{2,1,0:T(8,128)(2,1)S(1)}, bf16[4,512,128]{2,1,0:T(8,128)(2,1)S(1)}, ...), condition=%wide.region_12.12_spmd, body=%wide.region_9.11_spmd.sunk | while | flops 680328192 | bytes 17311820 | solution.py:47
  764.6 4.9 copy.56
  769.5 95.4 %all_to_all.51 = bf16[8,2048,128]{2,0,1:T(8,128)(2,1)S(1)} all-to-all(bf16[8,2048,128]{2,0,1:T(8,128)(2,1)S(1)} %copy.56), channel_id=1, replica_groups=mesh['groups'=2,'seq'=4,'adapt'=4] {'seq'}, dimensions={1} | all-to-all | bytes 8388608 | tf_op jit(solution)/shard_map/all_to_all | solution.py:119
  864.9 2.9 copy.58
  867.8 6.6 copy.59
  874.4 6.4 copy.60
  (139 shorter events, 92.5 us)
Async XLA Ops:
  7.4 1.8 copy-start
  7.4 182.9 %all-reduce.3.cloned.1.call-start = ((), (), s32[]{:S(2)}) async-start(), calls=%async_computation.4 | async-start | bytes 9437184 | tf_op jit(solution)/shard_map/psum | solution.py:86
  15.2 8.3 copy-start.2
  15.2 175.1 %all-gather.2.cloned.1.call-start = ((), (), s32[]{:S(2)}) async-start(), calls=%async_computation.3 | async-start | bytes 31457280 | tf_op jit(solution)/shard_map/all_gather | solution.py:90
  33.0 0.7 copy-start.4
  304.6 98.7 %all-to-all-start = ((bf16[32,512,128]{2,1,0:T(8,128)(2,1)}), bf16[32,512,128]{2,1,0:T(8,128)(2,1)}, u32[]{:S(2)}, u32[]{:S(2)}) async-start(bf16[32,512,128]{2,1,0:T(8,128)(2,1)} %bitcast.96), calls=%async_computation | async-start | bytes 8388608 | tf_op jit(solution)/shard_map/all_to_all | solution.py:115
  323.1 4.6 copy-start.3
  403.3 233.8 %all-to-all-start.1 = ((bf16[32,640,2,128]{3,1,2,0:T(8,128)(2,1)}), bf16[32,640,2,128]{3,1,2,0:T(8,128)(2,1)}, u32[]{:S(2)}, u32[]{:S(2)}) async-start(bf16[32,640,2,128]{3,1,2,0:T(8,128)(2,1)} %bitcast.94), calls=%async_computation.1 | async-start | bytes 20971520 | tf_op jit(solution)/shard_map/all_to_all | solution.py:116
  867.8 13.0 %copy-start.1 = (bf16[4,3072,64]{1,2,0:T(8,128)(2,1)S(1)}, bf16[4,3072,64]{1,2,0:T(8,128)(2,1)}, u32[]{:S(2)}) copy-start(bf16[4,3072,64]{1,2,0:T(8,128)(2,1)} %param.17) | copy-start | bytes 4718596
Sparse Core Ops, SparseCore 0:
  15.3 174.9 all-reduce.2
Sparse Core Ops, SparseCore 1:
  33.1 157.0 all-gather.1
where the time goes:
time: 891 us; the launch traced here: 888 us
  waiting for transfers between devices  417 us (47%)
  matrix products  141 us (16%)
  local copies, waits for them, and re-layouts  123 us (14%)
  blocking collectives  95.4 us (11%)
  other arithmetic  85 us (10%)
  between operations  15 us (2%)
  starting transfers between devices  11.2 us (1%)
    all_to_all x1, waiting for transfers between devices, on_device(): lax.all_to_all(joined, 'seq', split_axis=0, concat_axis=1, tiled=True)  223 us
    psum x1, waiting for transfers between devices, on_device(): lax.psum(up_terms, 'seq').astype(jnp.float32)  156 us
    all_to_all x1, blocking collectives, on_device(): lax.all_to_all(attended, 'seq', split_axis=1, concat_axis=0, tiled=True)  95.4 us
    dot_general x1, matrix products, on_device(): jnp.einsum('rtd,dc->rtc', block_rows, query_key_value_weight, preferred_e...  47.6 us
    all_to_all x1, waiting for transfers between devices, on_device(): lax.all_to_all(queries, 'seq', split_axis=0, concat_axis=1, tiled=True)  38.2 us
    dot_general x32, matrix products, one_block(): jnp.dot(weights.astype(jnp.bfloat16), value_rows, preferred_element_type=...  33.5 us
    dot_general x32, matrix products, one_block(): lax.dot_general(block_rows, key_rows, (((1,), (1,)), ((), ())), preferred...  29.7 us
    reduce_sum x32, other arithmetic, one_block(): weights = weights / jnp.sum(weights, axis=-1, keepdims=True)  27 us
  transfers between devices with their start and end apart: 4, of which 3 were waited for; matrix products, arithmetic and copies ran while one was open for 9% of the time, Pallas kernels for 0%

commit v1 on v0

--- a/solution.py
+++ b/solution.py
@@ -5,6 +5,29 @@
 from jax.sharding import PartitionSpec as P
 
 HEAD_SIZE = 128
+
+
+def split_up(array, dim, count):
+    shape = array.shape
+    parts = array.reshape(*shape[:dim], count, shape[dim] // count, *shape[dim + 1 :])
+    return jnp.moveaxis(parts, dim, 0)
+
+
+def in_order(tiles, dim):
+    tiles = jnp.moveaxis(tiles, 0, dim)
+    dims = tiles.shape
+    return tiles.reshape(*dims[:dim], dims[dim] * dims[dim + 1], *dims[dim + 2 :])
+
+
+def exchange_directly(value, axis, split_dim, concat_dim):
+    size, index = (lax.axis_size(axis), lax.axis_index(axis))
+    blocks = split_up(value, split_dim, size)
+    outs = [blocks[index]]
+    for step in range(1, size):
+        sent = blocks[(index + step) % size]
+        outs.append(lax.ppermute(sent, axis, [(i, (i + step) % size) for i in range(size)]))
+    blocks = jnp.stack(outs)[(index - jnp.arange(size)) % size]
+    return in_order(blocks, concat_dim)
 
 
 def layer_modulate(image, modulation):
@@ -113,7 +136,7 @@
     )
     query_items, joined_items = (
         lax.all_to_all(queries, "seq", split_axis=0, concat_axis=1, tiled=True),
-        lax.all_to_all(joined, "seq", split_axis=0, concat_axis=1, tiled=True),
+        exchange_directly(joined, "seq", 0, 1),
     )
     attended = lax.map(attend_item, (query_items, joined_items))
     returned = lax.all_to_all(attended, "seq", split_axis=1, concat_axis=0, tiled=True)

time: 891 us -> 935 us (1.049)
  waiting for transfers between devices: 417 us -> 354 us
  blocking collectives: 95.4 us -> 151 us
  local copies, waits for them, and re-layouts: 123 us -> 146 us
  other arithmetic: 85 us -> 107 us
    all_to_all x1 -> x0, waiting for transfers between devices: 223 us -> none  [on_device(): lax.all_to_all(joined, 'seq', split_axis=0, concat_axis=1, tiled=True)]
    ppermute x0 -> x3, waiting for transfers between devices: none -> 208 us  [exchange_directly(): lax.ppermute(sent, axis, [(i, (i + step) % size) for i in range(size)])]
    all_to_all x1, blocking collectives: 95.4 us -> 151 us  [on_device(): lax.all_to_all(attended, 'seq', split_axis=1, concat_axis=0, tiled=True)]
    all_to_all x1, waiting for transfers between devices: 38.2 us -> 0.01 us  [on_device(): lax.all_to_all(queries, 'seq', split_axis=0, concat_axis=1, tiled=True)]
    gather x0 -> x3, local copies, waits for them, and re-layouts: none -> 15.1 us  [exchange_directly(): blocks = jnp.stack(outs)[(index - jnp.arange(size)) % size]]
    transpose x0 -> x1, other arithmetic: none -> 12.1 us  [in_order(): tiles = jnp.moveaxis(tiles, 0, dim)]
  transfers between devices with their start and end apart: 4 -> 6, of which waited for: 3 -> 3; matrix products, arithmetic and copies ran while one was open for 9% -> 13% of each run, Pallas kernels for 0% -> 0%
where the time goes in v1:
time: 935 us; the launch traced here: 926 us
  waiting for transfers between devices  354 us (38%)
  blocking collectives  151 us (16%)
  local copies, waits for them, and re-layouts  146 us (16%)
  matrix products  141 us (15%)
  other arithmetic  107 us (11%)
  between operations  15.3 us (2%)
  starting transfers between devices  10.8 us (1%)
    ppermute x3, waiting for transfers between devices, exchange_directly(): lax.ppermute(sent, axis, [(i, (i + step) % size) for i in range(size)])  208 us
    all_to_all x1, blocking collectives, on_device(): lax.all_to_all(attended, 'seq', split_axis=1, concat_axis=0, tiled=True)  151 us
    psum x1, waiting for transfers between devices, on_device(): lax.psum(up_terms, 'seq').astype(jnp.float32)  147 us
    dot_general x1, matrix products, on_device(): jnp.einsum('rtd,dc->rtc', block_rows, query_key_value_weight, preferred_e...  47.6 us
    dot_general x32, matrix products, one_block(): jnp.dot(weights.astype(jnp.bfloat16), value_rows, preferred_element_type=...  33.5 us
    dot_general x32, matrix products, one_block(): lax.dot_general(block_rows, key_rows, (((1,), (1,)), ((), ())), preferred...  29.7 us
    reduce_sum x32, other arithmetic, one_block(): weights = weights / jnp.sum(weights, axis=-1, keepdims=True)  27 us
    add x1, local copies, waits for them, and re-layouts, on_device(): frozen + jnp.einsum('rtk,rkc->rtc', shrunk, up_fetched, preferred_element...  24.8 us
  transfers between devices with their start and end apart: 6, of which 3 were waited for; matrix products, arithmetic and copies ran while one was open for 13% of the time, Pallas kernels for 0%

profile of v1, /device:TPU:0, one launch (start us, length us, event | category | flops | bytes accessed | tf_op | source)
XLA Modules:
  0.0 926.0 jit_solution(8158428505150302863)
XLA Ops:
  9.2 2.8 convolution_convert_fusion
  12.1 3.1 convolution_convert_fusion.1
  15.2 3.7 convert_reduce_fusion
  18.9 4.5 fusion.10
  23.6 9.4 %fusion.13 = bf16[2,512,3072]{2,1,0:T(8,128)(2,1)} fusion(bf16[2,512,3072]{2,1,0:T(8,128)(2,1)} %param.14, f32[2,3072]{1,0:T(2,128)S(1)} %get-tuple-element.87, f32[2,512]{1,0:T(2,128)S(1)} %add_rsqrt_fusion.2, f32[2,512]{1,0:T(2,128)S(1)} %broadcast_multiply_fusion, f32[2,3072]{1,0:T(2,128)S(1)} %get-tuple-element.88), kind=kLoop, calls=%fused_computation.26 | loop fusion | flops 18874368 | bytes 12640256 | tf_op jit(solution)/shard_map/convert_element_type | solution.py:38
  33.0 6.6 copy.52
  39.7 3.2 copy.79
  43.4 146.9 %all-reduce.3.cloned.1.call-done = (bf16[8,64,1536]{2,0,1:T(8,128)(2,1)}, bf16[8,3072,64]{1,0,2:T(8,128)(2,1)}) async-done(((bf16[8,64,1536]{2,0,1:T(8,128)(2,1)}, bf16[8,3072,64]{1,0,2:T(8,128)(2,1)}), (bf16[8,64,1536]{2,0,1:T(8,128)(2,1)}, bf16[8,3072,64]{1,0,2:T(8,128)(2,1)})) %all-reduce.3.cloned.1.call-update) | async-done | bytes 4718608 | tf_op jit(solution)/shard_map/psum | solution.py:109
  190.3 23.9 %fusion.18 = f32[8,512,1536]{2,1,0:T(8,128)} fusion(bf16[8,64,1536]{2,0,1:T(8,128)(2,1)} %get-tuple-element.73, bf16[8,512,3072]{2,1,0:T(8,128)(2,1)} %all-gather.2.cloned.1.call-done, bf16[8,3072,64]{1,0,2:T(8,128)(2,1)} %get-tuple-element.74), kind=kOutput, calls=%fused_computation.48 | convolution fusion | flops 2416181248 | bytes 55050240 | tf_op jit(solution)/shard_map/rtk,rkc->rtc/dot_general | solution.py:120
  214.2 47.6 %convolution_add_fusion = f32[8,512,1536]{2,1,0:T(8,128)} fusion(f32[8,512,1536]{2,1,0:T(8,128)} %fusion.18, bf16[8,512,3072]{2,1,0:T(8,128)(2,1)} %all-gather.2.cloned.1.call-done, bf16[3072,1536]{1,0:T(8,128)(2,1)} %param.16), kind=kOutput, calls=%fused_computation.18 | convolution fusion | flops 38660997120 | bytes 84934656 | tf_op jit(solution)/shard_map/rtd,dc->rtc/dot_general | solution.py:117
  261.8 24.8 %copy.49 = f32[8,512,1536]{1,2,0:T(8,128)} copy(f32[8,512,1536]{2,1,0:T(8,128)} %convolution_add_fusion) | data formatting | bytes 50331648 | tf_op jit(solution)/shard_map/add | solution.py:120
  286.7 4.6 multiply_reduce_fusion
  291.2 4.6 multiply_reduce_fusion.1
  295.8 7.0 fusion.15
  302.8 6.5 copy.50
  309.3 4.9 all-to-all-start
  314.3 4.0 slice.59
  318.3 7.0 multiply_convert_fusion
  325.3 6.2 maximum_bitcast_fusion.1
  331.5 9.1 pad_maximum_fusion
  340.6 15.1 %copy.54 = bf16[8,4,640,2,128]{4,2,3,1,0:T(8,128)(2,1)} copy(bf16[8,4,640,2,128]{2,4,3,1,0:T(8,128)(2,1)} %pad_maximum_fusion) | data formatting | bytes 20971520 | tf_op jit(solution)/shard_map/concatenate | solution.py:132
  355.7 8.3 constant_dynamic-slice_fusion.1
  364.0 2.0 collective-permute-start
  366.0 2.4 collective-permute-start.1
  368.3 1.5 collective-permute-start.2
  369.8 73.8 %collective-permute-done = bf16[8,640,2,128]{3,1,2,0:T(8,128)(2,1)} collective-permute-done((bf16[8,640,2,128]{3,1,2,0:T(8,128)(2,1)}, bf16[8,640,2,128]{3,1,2,0:T(8,128)(2,1)}, u32[]{:S(2)}, u32[]{:S(2)}) %collective-permute-start) | collective-permute-done | bytes 2621472 | tf_op jit(solution)/shard_map/ppermute | solution.py:28
  443.6 133.8 %collective-permute-done.1 = bf16[8,640,2,128]{3,1,2,0:T(8,128)(2,1)} collective-permute-done((bf16[8,640,2,128]{3,1,2,0:T(8,128)(2,1)}, bf16[8,640,2,128]{3,1,2,0:T(8,128)(2,1)}, u32[]{:S(2)}, u32[]{:S(2)}) %collective-permute-start.1) | collective-permute-done | bytes 2621472 | tf_op jit(solution)/shard_map/ppermute | solution.py:28
  577.4 5.8 pad_maximum_fusion.1
  583.2 3.1 mini-gather-slice.2
  586.2 6.8 gather_fusion
  593.0 4.1 pad_maximum_fusion.2
  597.2 5.2 gather_fusion.1
  602.4 12.1 %maximum_bitcast_fusion = bf16[8,4,640,2,128]{4,2,3,0,1:T(8,128)(2,1)} fusion(bf16[4,8,256,2,128]{4,2,3,1,0:T(8,128)(2,1)} %gather_fusion.1, bf16[4,8,384,2,128]{4,2,3,1,0:T(8,128)(2,1)} %gather_fusion), kind=kLoop, calls=%fused_computation.29 | loop fusion | flops 20971520 | bytes 20971520 | tf_op jit(solution)/shard_map/transpose | solution.py:17
  614.5 9.2 copy.55
  623.7 4.7 copy.51
  628.4 118.3 %while.21 = (s32[]{:T(128)}, bf16[8,2048,128]{2,1,0:T(8,128)(2,1)}, bf16[8,2048,128]{2,1,0:T(8,128)(2,1)}, bf16[8,2560,2,128]{3,1,2,0:T(8,128)(2,1)}, s32[]{:T(128)}, /*index=5*/s32[]{:T(128)}, s32[]{:T(128)}) while((s32[]{:T(128)}, bf16[8,2048,128]{2,1,0:T(8,128)(2,1)}, bf16[8,2048,128]{2,1,0:T(8,128)(2,1)}, ...), condition=%wide.region_13.14_spmd, body=%wide.region_8.13_spmd.sunk | while | flops 680328192 | bytes 24652504 | solution.py:141
  628.4 1.4 dynamic-slice_bitcast_fusion.5
  629.9 1.1 constant_dynamic-slice_fusion.3
  631.0 11.4 %while.22 = (s32[]{:T(128)}, bf16[4,512,128]{2,1,0:T(8,128)(2,1)S(1)}, bf16[4,512,128]{2,1,0:T(8,128)(2,1)S(1)}, bf16[2560,128]{1,0:T(8,128)(2,1)S(1)}, bf16[2560,128]{1,0:T(8,128)(2,1)S(1)}, /*index=5*/s32[]{:T(128)}) while((s32[]{:T(128)}, bf16[4,512,128]{2,1,0:T(8,128)(2,1)S(1)}, bf16[4,512,128]{2,1,0:T(8,128)(2,1)S(1)}, ...), condition=%wide.region_12.12_spmd, body=%wide.region_9.11_spmd.sunk | while | flops 680328192 | bytes 17311820 | solution.py:70
  643.2 1.4 dynamic-slice_bitcast_fusion.5
  644.7 1.1 constant_dynamic-slice_fusion.3
  645.8 11.4 %while.22 = (s32[]{:T(128)}, bf16[4,512,128]{2,1,0:T(8,128)(2,1)S(1)}, bf16[4,512,128]{2,1,0:T(8,128)(2,1)S(1)}, bf16[2560,128]{1,0:T(8,128)(2,1)S(1)}, bf16[2560,128]{1,0:T(8,128)(2,1)S(1)}, /*index=5*/s32[]{:T(128)}) while((s32[]{:T(128)}, bf16[4,512,128]{2,1,0:T(8,128)(2,1)S(1)}, bf16[4,512,128]{2,1,0:T(8,128)(2,1)S(1)}, ...), condition=%wide.region_12.12_spmd, body=%wide.region_9.11_spmd.sunk | while | flops 680328192 | bytes 17311820 | solution.py:70
  658.0 1.4 dynamic-slice_bitcast_fusion.5
  659.5 1.1 constant_dynamic-slice_fusion.3
  660.6 11.4 %while.22 = (s32[]{:T(128)}, bf16[4,512,128]{2,1,0:T(8,128)(2,1)S(1)}, bf16[4,512,128]{2,1,0:T(8,128)(2,1)S(1)}, bf16[2560,128]{1,0:T(8,128)(2,1)S(1)}, bf16[2560,128]{1,0:T(8,128)(2,1)S(1)}, /*index=5*/s32[]{:T(128)}) while((s32[]{:T(128)}, bf16[4,512,128]{2,1,0:T(8,128)(2,1)S(1)}, bf16[4,512,128]{2,1,0:T(8,128)(2,1)S(1)}, ...), condition=%wide.region_12.12_spmd, body=%wide.region_9.11_spmd.sunk | while | flops 680328192 | bytes 17311820 | solution.py:70
  672.8 1.4 dynamic-slice_bitcast_fusion.5
  674.3 1.1 constant_dynamic-slice_fusion.3
  675.4 11.4 %while.22 = (s32[]{:T(128)}, bf16[4,512,128]{2,1,0:T(8,128)(2,1)S(1)}, bf16[4,512,128]{2,1,0:T(8,128)(2,1)S(1)}, bf16[2560,128]{1,0:T(8,128)(2,1)S(1)}, bf16[2560,128]{1,0:T(8,128)(2,1)S(1)}, /*index=5*/s32[]{:T(128)}) while((s32[]{:T(128)}, bf16[4,512,128]{2,1,0:T(8,128)(2,1)S(1)}, bf16[4,512,128]{2,1,0:T(8,128)(2,1)S(1)}, ...), condition=%wide.region_12.12_spmd, body=%wide.region_9.11_spmd.sunk | while | flops 680328192 | bytes 17311820 | solution.py:70
  687.6 1.4 dynamic-slice_bitcast_fusion.5
  689.1 1.1 constant_dynamic-slice_fusion.3
  690.2 11.4 %while.22 = (s32[]{:T(128)}, bf16[4,512,128]{2,1,0:T(8,128)(2,1)S(1)}, bf16[4,512,128]{2,1,0:T(8,128)(2,1)S(1)}, bf16[2560,128]{1,0:T(8,128)(2,1)S(1)}, bf16[2560,128]{1,0:T(8,128)(2,1)S(1)}, /*index=5*/s32[]{:T(128)}) while((s32[]{:T(128)}, bf16[4,512,128]{2,1,0:T(8,128)(2,1)S(1)}, bf16[4,512,128]{2,1,0:T(8,128)(2,1)S(1)}, ...), condition=%wide.region_12.12_spmd, body=%wide.region_9.11_spmd.sunk | while | flops 680328192 | bytes 17311820 | solution.py:70
  702.4 1.4 dynamic-slice_bitcast_fusion.5
  703.9 1.1 constant_dynamic-slice_fusion.3
  705.0 11.4 %while.22 = (s32[]{:T(128)}, bf16[4,512,128]{2,1,0:T(8,128)(2,1)S(1)}, bf16[4,512,128]{2,1,0:T(8,128)(2,1)S(1)}, bf16[2560,128]{1,0:T(8,128)(2,1)S(1)}, bf16[2560,128]{1,0:T(8,128)(2,1)S(1)}, /*index=5*/s32[]{:T(128)}) while((s32[]{:T(128)}, bf16[4,512,128]{2,1,0:T(8,128)(2,1)S(1)}, bf16[4,512,128]{2,1,0:T(8,128)(2,1)S(1)}, ...), condition=%wide.region_12.12_spmd, body=%wide.region_9.11_spmd.sunk | while | flops 680328192 | bytes 17311820 | solution.py:70
  717.2 1.4 dynamic-slice_bitcast_fusion.5
  719.8 11.4 %while.22 = (s32[]{:T(128)}, bf16[4,512,128]{2,1,0:T(8,128)(2,1)S(1)}, bf16[4,512,128]{2,1,0:T(8,128)(2,1)S(1)}, bf16[2560,128]{1,0:T(8,128)(2,1)S(1)}, bf16[2560,128]{1,0:T(8,128)(2,1)S(1)}, /*index=5*/s32[]{:T(128)}) while((s32[]{:T(128)}, bf16[4,512,128]{2,1,0:T(8,128)(2,1)S(1)}, bf16[4,512,128]{2,1,0:T(8,128)(2,1)S(1)}, ...), condition=%wide.region_12.12_spmd, body=%wide.region_9.11_spmd.sunk | while | flops 680328192 | bytes 17311820 | solution.py:70
  731.9 1.4 dynamic-slice_bitcast_fusion.5
  733.4 1.1 constant_dynamic-slice_fusion.3
  734.5 11.4 %while.22 = (s32[]{:T(128)}, bf16[4,512,128]{2,1,0:T(8,128)(2,1)S(1)}, bf16[4,512,128]{2,1,0:T(8,128)(2,1)S(1)}, bf16[2560,128]{1,0:T(8,128)(2,1)S(1)}, bf16[2560,128]{1,0:T(8,128)(2,1)S(1)}, /*index=5*/s32[]{:T(128)}) while((s32[]{:T(128)}, bf16[4,512,128]{2,1,0:T(8,128)(2,1)S(1)}, bf16[4,512,128]{2,1,0:T(8,128)(2,1)S(1)}, ...), condition=%wide.region_12.12_spmd, body=%wide.region_9.11_spmd.sunk | while | flops 680328192 | bytes 17311820 | solution.py:70
  746.7 4.9 copy.56
  751.6 150.7 %all_to_all.33 = bf16[8,2048,128]{2,0,1:T(8,128)(2,1)S(1)} all-to-all(bf16[8,2048,128]{2,0,1:T(8,128)(2,1)S(1)} %copy.56), channel_id=1, replica_groups=mesh['groups'=2,'seq'=4,'adapt'=4] {'seq'}, dimensions={1} | all-to-all | bytes 8388608 | tf_op jit(solution)/shard_map/all_to_all | solution.py:142
  902.3 2.9 copy.58
  905.3 6.6 copy.59
  911.9 6.4 copy.60
  (152 shorter events, 101.3 us)
Async XLA Ops:
  7.4 1.8 copy-start
  7.4 182.9 %all-reduce.3.cloned.1.call-start = ((), (), s32[]{:S(2)}) async-start(), calls=%async_computation.3 | async-start | bytes 9437184 | tf_op jit(solution)/shard_map/psum | solution.py:109
  15.1 8.3 copy-start.2
  15.2 175.1 %all-gather.2.cloned.1.call-start = ((), (), s32[]{:S(2)}) async-start(), calls=%async_computation.2 | async-start | bytes 31457280 | tf_op jit(solution)/shard_map/all_gather | solution.py:113
  33.0 10.0 %copy-start.4 = (f32[2,128]{1,0:T(2,128)S(1)}, f32[2,128]{1,0:T(2,128)}, u32[]{:S(2)}) copy-start(f32[2,128]{1,0:T(2,128)} %param.23) | copy-start | bytes 3076
  309.3 314.4 %all-to-all-start = ((bf16[32,512,128]{2,1,0:T(8,128)(2,1)}), bf16[32,512,128]{2,1,0:T(8,128)(2,1)}, u32[]{:S(2)}, u32[]{:S(2)}) async-start(bf16[32,512,128]{2,1,0:T(8,128)(2,1)} %bitcast.106), calls=%async_computation | async-start | bytes 8388608 | tf_op jit(solution)/shard_map/all_to_all | solution.py:138
  314.2 4.1 copy-start.3
  364.0 79.6 %collective-permute-start = (bf16[8,640,2,128]{3,1,2,0:T(8,128)(2,1)}, bf16[8,640,2,128]{3,1,2,0:T(8,128)(2,1)}, u32[]{:S(2)}, u32[]{:S(2)}) collective-permute-start(bf16[8,640,2,128]{3,1,2,0:T(8,128)(2,1)} %get-tuple-element.82), channel_id=1, source_target_pairs={{0,4},{4,8},{8,12},{12,0},{1,5},{5,9},{9,13},{13,1},{2,6},{6,10},{... | collective-permute-start | bytes 7864328 | tf_op jit(solution)/shard_map/ppermute | solution.py:28
  366.0 211.4 %collective-permute-start.1 = (bf16[8,640,2,128]{3,1,2,0:T(8,128)(2,1)}, bf16[8,640,2,128]{3,1,2,0:T(8,128)(2,1)}, u32[]{:S(2)}, u32[]{:S(2)}) collective-permute-start(bf16[8,640,2,128]{3,1,2,0:T(8,128)(2,1)} %get-tuple-element.81), channel_id=1, source_target_pairs={{0,8},{4,12},{8,0},{12,4},{1,9},{5,13},{9,1},{13,5},{2,10},{6,14},... | collective-permute-start | bytes 7864328 | tf_op jit(solution)/shard_map/ppermute | solution.py:28
  368.3 209.1 %collective-permute-start.2 = (bf16[8,640,2,128]{3,1,2,0:T(8,128)(2,1)}, bf16[8,640,2,128]{3,1,2,0:T(8,128)(2,1)}, u32[]{:S(2)}, u32[]{:S(2)}) collective-permute-start(bf16[8,640,2,128]{3,1,2,0:T(8,128)(2,1)} %get-tuple-element.80), channel_id=1, source_target_pairs={{0,12},{4,0},{8,4},{12,8},{1,13},{5,1},{9,5},{13,9},{2,14},{6,2},{... | collective-permute-start | bytes 7864328 | tf_op jit(solution)/shard_map/ppermute | solution.py:28
  905.3 13.0 %copy-start.1 = (bf16[4,3072,64]{1,2,0:T(8,128)(2,1)S(1)}, bf16[4,3072,64]{1,2,0:T(8,128)(2,1)}, u32[]{:S(2)}) copy-start(bf16[4,3072,64]{1,2,0:T(8,128)(2,1)} %param.17) | copy-start | bytes 4718596
Sparse Core Ops, SparseCore 0:
  15.3 174.9 all-reduce.2
Sparse Core Ops, SparseCore 1:
  33.1 157.0 all-gather.1
